TPU v7x, 32 devices: a whole 2x2x4 slice. The times are simulated.
32 devices in a mesh: row: 4 (over z), col: 8 (over y, x, core).
Axes of the slice: x: 2, y: 2, z: 4, core: 2. Of those that a mesh axis runs over, the one named last changes fastest.
Arguments:
- front: float32 [8192, 8192], P('row', 'col'), may hold values from -6 to 6
- inverses: float32 [2, 512, 512], replicated, may hold values from -2 to 2, as said below
- block_owner: int32 [64, 64], P('row', 'col'), may hold values from -1 to 31, as said below
- block_slot: int32 [64, 64], P('row', 'col'), may hold values from 0 to 47
- parent_in: float32 [1536, 128, 128], P(('row', 'col')), may hold values from -6 to 6
Outputs:
- updated: float32 [8192, 8192], P('row', 'col')
- panels: float32 [8192, 1024], P(('row', 'col'))
- parent_out: float32 [1536, 128, 128], P(('row', 'col'))
Inputs may be any that keep to these rules, and one draw needn't show every extreme that they name: Entries of the pivot block inverses. `block_owner`: -1 exactly for blocks above the diagonal (I < J); on one device's 16 x 8 blocks no device is named more than 4 times, and on some device some device is named exactly 4 times.
All inputs are finite; a program needn't handle non-finite values.
Results may differ from a plain program's by a relative error of at most 0.00014.
Values sent between devices are 32-bit elements; how exact they have to be, the bound alone decides.
A program may use at most 128 MiB of HBM per device.

v0:
```python
import jax
import jax.numpy as jnp
from jax import lax
from jax.sharding import PartitionSpec as P


def spread_2(block, axis, source):
    block = jnp.where(lax.axis_index(axis) == source, block, jnp.zeros_like(block))
    return lax.psum(block, axis)


def matmul(left_side, right_side):
    return jnp.dot(
        left_side, right_side, preferred_element_type=jnp.float32, precision=lax.Precision.HIGHEST
    )


def spread(columns, rows):
    columns = spread_2(columns, "col", 0)
    rows = spread_2(rows, "row", 0)
    return (columns, rows)


def local(front, inverses, block_owner, block_slot, parent_in):
    panel_width = inverses.shape[1]
    columns_one, rows_one = spread(front[:, 0:panel_width], front[0:panel_width, :])
    factor_one = matmul(columns_one, inverses[0])
    partial_value = front - matmul(factor_one, rows_one)
    columns_two, rows_two = spread(
        partial_value[:, panel_width : 2 * panel_width],
        partial_value[panel_width : 2 * panel_width, :],
    )
    factor_two = matmul(columns_two, inverses[1])
    factors = jnp.concatenate([factor_one, factor_two], axis=1)
    updated = partial_value - matmul(factor_two, rows_two)
    piece_rows = factors.shape[0] // lax.axis_size("col")
    panels = lax.dynamic_slice_in_dim(factors, lax.axis_index("col") * piece_rows, piece_rows, 0)
    block_rows, block_cols = block_owner.shape
    block_edge = parent_in.shape[1]
    held = parent_in.shape[0]
    block_count = block_rows * block_cols
    row_devices = lax.axis_size("row")
    col_devices = lax.axis_size("col")
    devices = row_devices * col_devices
    capacity = max(1, (block_count + devices - 1) // devices)
    blocks = updated.reshape(block_rows, block_edge, block_cols, block_edge).transpose(0, 2, 1, 3)
    blocks = blocks.reshape(block_count, block_edge, block_edge)
    owners = block_owner.reshape(block_count)
    parent_slots = block_slot.reshape(block_count)
    position = jnp.arange(block_count, dtype=jnp.int32)
    earlier = (owners[:, None] == owners[None, :]) & (position[None, :] < position[:, None])
    within = jnp.sum(earlier.astype(jnp.int32), axis=1)
    target = jnp.where(owners >= 0, owners * capacity + within, devices * capacity)
    outgoing = (
        jnp.zeros((devices * capacity, block_edge, block_edge), jnp.float32)
        .at[target]
        .set(blocks, mode="drop")
    )
    labels = (
        jnp.full((devices * capacity,), held, jnp.float32)
        .at[target]
        .set(parent_slots.astype(jnp.float32), mode="drop")
    )
    arrived, markers = (
        lax.all_to_all(
            outgoing.reshape(devices, capacity, block_edge, block_edge),
            ("row", "col"),
            split_axis=0,
            concat_axis=0,
            tiled=True,
        ),
        lax.all_to_all(
            labels.reshape(devices, capacity),
            ("row", "col"),
            split_axis=0,
            concat_axis=0,
            tiled=True,
        ),
    )
    arrived = arrived.reshape(devices * capacity, block_edge, block_edge)
    markers = markers.reshape(devices * capacity).astype(jnp.int32)
    added = jnp.zeros(parent_in.shape, jnp.float32).at[markers].add(arrived, mode="drop")
    parent_out = parent_in + added
    return (updated, panels, parent_out)


def solution(mesh):
    in_specs = (
        P("row", "col"),
        P(),
        P("row", "col"),
        P("row", "col"),
        P(("row", "col"), None, None),
    )
    out_specs = (P("row", "col"), P(("row", "col"), None), P(("row", "col"), None, None))
    return jax.shard_map(local, mesh=mesh, in_specs=in_specs, out_specs=out_specs, check_vma=False)
```

profile of v0, /device:TPU:7, one launch (start us, length us, event | category | flops | bytes accessed | tf_op | source)
XLA Modules:
  0.0 641.1 jit_solution(14133104792628374288)
XLA Ops:
  7.2 0.0 all-reduce.5.cloned.1.call-start
  7.2 4.7 slice_select_fusion.1
  11.9 0.0 all-reduce.5.cloned.1.call-update
  11.9 0.0 copy-start.4
  12.0 0.0 all-reduce.7.cloned.1.call-start
  12.0 3.3 slice_select_fusion.3
  15.3 0.0 all-reduce.7.cloned.1.call-update
  15.4 0.0 all-reduce.9.cloned.1.call-start
  15.4 77.7 %all-reduce.5.cloned.1.call-done = f32[2048,512]{1,0:T(8,128)} async-done(((f32[2048,512]{1,0:T(8,128)}), f32[2048,512]{1,0:T(8,128)}) %all-reduce.5.cloned.1.call-update) | async-done | bytes 4194320 | tf_op jit(solution)/shard_map/psum | solution.py:9
  93.1 0.0 copy-done.4
  93.2 10.0 %fusion.3 = f32[2048,512]{0,1:T(8,128)} fusion(f32[2048,512]{1,0:T(8,128)} %all-reduce.5.cloned.1.call-done, f32[2,512,512]{2,1,0:T(8,128)S(1)} %copy-done.4), kind=kOutput, calls=%fused_computation.14 | convolution fusion | flops 6442450944 | bytes 9437184 | tf_op jit(solution)/shard_map/dot_general | solution.py:13
  103.1 79.8 %all-reduce.7.cloned.1.call-done = f32[512,1024]{1,0:T(8,128)} async-done(((f32[512,1024]{1,0:T(8,128)}), f32[512,1024]{1,0:T(8,128)}) %all-reduce.7.cloned.1.call-update) | async-done | bytes 2097168 | tf_op jit(solution)/shard_map/psum | solution.py:9
  182.9 16.6 %convolution_subtract_fusion.1 = f32[2048,1024]{1,0:T(8,128)S(1)} fusion(f32[2048,1024]{1,0:T(8,128)} %param.5, f32[2048,512]{0,1:T(8,128)} %fusion.3, f32[512,1024]{1,0:T(8,128)} %all-reduce.7.cloned.1.call-done), kind=kOutput, calls=%fused_computation.8 | convolution fusion | flops 12886999040 | bytes 23068672 | tf_op jit(solution)/shard_map/dot_general | solution.py:13
  199.5 0.0 copy-start
  199.5 3.4 copy-done
  202.9 2.7 slice_select_fusion
  205.6 0.0 all-reduce.9.cloned.1.call-update
  205.6 0.0 copy-start.5
  205.6 0.0 copy-start.6
  205.6 0.0 all-reduce.11.cloned.1.call-start
  205.7 3.2 slice_select_fusion.2
  208.9 0.0 all-reduce.11.cloned.1.call-update
  208.9 0.0 copy-done.5
  208.9 0.1 copy.28
  209.0 0.1 copy.26
  209.1 0.1 ge.14
  209.2 0.0 copy-done.6
  209.2 0.1 copy.29
  209.3 0.1 reshape.99
  209.4 0.1 copy.27
  209.5 0.1 mul.22
  209.5 0.1 eq.25
  209.6 0.2 convert_reduce_fusion
  209.8 1.0 scatter_custom_fusion
  210.8 0.7 all_to_all.9
  211.5 4.6 all-to-all-start
  216.1 69.2 %all-reduce.9.cloned.1.call-done = f32[2048,512]{1,0:T(8,128)} async-done(((f32[2048,512]{1,0:T(8,128)}), f32[2048,512]{1,0:T(8,128)}) %all-reduce.9.cloned.1.call-update) | async-done | bytes 4194320 | tf_op jit(solution)/shard_map/psum | solution.py:9
  285.3 10.0 %fusion.1 = f32[2048,512]{0,1:T(8,128)} fusion(f32[2048,512]{1,0:T(8,128)} %all-reduce.9.cloned.1.call-done, f32[2,512,512]{2,1,0:T(8,128)S(1)} %copy-done.4), kind=kOutput, calls=%fused_computation.12 | convolution fusion | flops 6442450944 | bytes 9437184 | tf_op jit(solution)/shard_map/dot_general | solution.py:13
  295.3 79.7 %all-reduce.11.cloned.1.call-done = f32[512,1024]{1,0:T(8,128)} async-done(((f32[512,1024]{1,0:T(8,128)}), f32[512,1024]{1,0:T(8,128)}) %all-reduce.11.cloned.1.call-update) | async-done | bytes 2097168 | tf_op jit(solution)/shard_map/psum | solution.py:9
  374.9 16.8 %convolution_subtract_fusion = f32[2048,1024]{1,0:T(8,128)S(1)} fusion(f32[2048,1024]{1,0:T(8,128)} %copy-done, f32[2048,512]{0,1:T(8,128)} %fusion.1, f32[512,1024]{1,0:T(8,128)} %all-reduce.11.cloned.1.call-done), kind=kOutput, calls=%fused_computation.7 | convolution fusion | flops 12886999040 | bytes 23068672 | tf_op jit(solution)/shard_map/dot_general | solution.py:13
  391.7 0.0 copy-start.3
  391.7 2.2 copy.33
  393.9 1.5 copy-done.3
  395.4 4.7 copy.31
  400.1 4.3 broadcast_in_dim.18
  404.4 20.8 %scatter_fusion = f32[128,128,128]{2,1,0:T(8,128)} fusion(f32[128,128,128]{2,1,0:T(8,128)} %broadcast_in_dim.18, s32[128]{0:T(128)S(1)} %fusion.8, f32[128,128,128]{2,1,0:T(8,128)} %bitcast.35), kind=kCustom, calls=%fused_computation.1 | custom fusion | bytes 25166336 | tf_op jit(solution)/shard_map/scatter | solution.py:57
  425.2 0.0 all-to-all-done
  425.3 6.8 %all-to-all-start.1 = ((f32[32,4,128,128]{3,2,1,0:T(8,128)}), f32[32,4,128,128]{3,2,1,0:T(8,128)}, u32[]{:S(2)}, u32[]{:S(2)}) async-start(f32[32,4,128,128]{3,2,1,0:T(8,128)} %bitcast.33), calls=%async_computation.1 | async-start | bytes 16777216 | tf_op jit(solution)/shard_map/all_to_all | solution.py:65
  432.0 0.1 convert_reduce_fusion.1
  432.1 0.1 convert_element_type.26
  432.2 0.0 copy-start.2
  432.2 2.4 fusion
  434.6 2.5 copy.32
  437.2 178.7 %all-to-all-done.1 = f32[32,4,128,128]{3,2,1,0:T(8,128)} async-done(((f32[32,4,128,128]{3,2,1,0:T(8,128)}), f32[32,4,128,128]{3,2,1,0:T(8,128)}, u32[]{:S(2)}, u32[]{:S(2)}) %all-to-all-start.1) | async-done | bytes 8388640 | tf_op jit(solution)/shard_map/all_to_all | solution.py:65
  615.8 0.0 copy-done.2
  615.8 17.0 %scatter_fusion.1 = f32[48,128,128]{2,1,0:T(8,128)S(1)} fusion(f32[48,128,128]{2,1,0:T(8,128)S(1)} %copy-done.2, s32[128]{0:T(128)S(1)} %fusion.9, f32[128,128,128]{2,1,0:T(8,128)} %bitcast.9), kind=kCustom, calls=%fused_computation.2 | custom fusion | flops 2097152 | bytes 25166336 | tf_op jit(solution)/shard_map/scatter-add | solution.py:82
  632.9 0.0 copy-start.1
  632.9 1.7 copy-done.1
  (5 shorter events, 0.0 us)
Async XLA Ops:
  7.2 86.0 %all-reduce.5.cloned.1.call-start = ((), (), s32[]{:S(2)}) async-start(), calls=%async_computation.2 | async-start | bytes 8388608 | tf_op jit(solution)/shard_map/psum | solution.py:9
  11.9 81.2 %copy-start.4 = (f32[2,512,512]{2,1,0:T(8,128)S(1)}, f32[2,512,512]{2,1,0:T(8,128)}, u32[]{:S(2)}) copy-start(f32[2,512,512]{2,1,0:T(8,128)} %param.6) | copy-start | bytes 6291460
  12.0 171.0 %all-reduce.7.cloned.1.call-start = ((), (), s32[]{:S(2)}) async-start(), calls=%async_computation.3 | async-start | bytes 4194304 | tf_op jit(solution)/shard_map/psum | solution.py:9
  15.4 269.9 %all-reduce.9.cloned.1.call-start = ((), (), s32[]{:S(2)}) async-start(), calls=%async_computation.4 | async-start | bytes 8388608 | tf_op jit(solution)/shard_map/psum | solution.py:9
  199.5 3.4 copy-start
  205.6 3.3 copy-start.5
  205.6 3.6 copy-start.6
  205.6 169.3 %all-reduce.11.cloned.1.call-start = ((), (), s32[]{:S(2)}) async-start(), calls=%async_computation.5 | async-start | bytes 4194304 | tf_op jit(solution)/shard_map/psum | solution.py:9
  211.5 213.7 %all-to-all-start = ((f32[32,1,4]{2,1,0:T(1,128)}), f32[32,1,4]{2,1,0:T(1,128)S(1)}, u32[]{:S(2)}, u32[]{:S(2)}) async-start(f32[32,1,4]{2,1,0:T(1,128)} %bitcast.4), calls=%async_computation | async-start | bytes 32768 | tf_op jit(solution)/shard_map/all_to_all | solution.py:72
  391.7 3.7 copy-start.3
  425.3 190.6 %all-to-all-start.1 = ((f32[32,4,128,128]{3,2,1,0:T(8,128)}), f32[32,4,128,128]{3,2,1,0:T(8,128)}, u32[]{:S(2)}, u32[]{:S(2)}) async-start(f32[32,4,128,128]{3,2,1,0:T(8,128)} %bitcast.33), calls=%async_computation.1 | async-start | bytes 16777216 | tf_op jit(solution)/shard_map/all_to_all | solution.py:65
  432.2 183.6 %copy-start.2 = (f32[48,128,128]{2,1,0:T(8,128)S(1)}, f32[48,128,128]{2,1,0:T(8,128)}, u32[]{:S(2)}) copy-start(f32[48,128,128]{2,1,0:T(8,128)} %param.9) | copy-start | bytes 9437188
  632.9 1.7 copy-start.1
Sparse Core Ops, SparseCore 0:
  12.1 81.0 all-reduce.4
  96.1 86.7 all-reduce.6
  205.7 79.5 all-reduce.8
  288.1 86.7 all-reduce.10
where the time goes:
time: 645 us; the launch traced here: 641 us
  waiting for transfers between devices  485 us (75%)
  matrix products  53.3 us (8%)
  local copies, waits for them, and re-layouts  43.6 us (7%)
  other arithmetic  33.6 us (5%)
  between operations  14 us (2%)
  starting transfers between devices  11.5 us (2%)
    psum x4, waiting for transfers between devices, spread_2(): return lax.psum(block, axis)  306 us
    all_to_all x1, waiting for transfers between devices, local(): lax.all_to_all(outgoing.reshape(devices, capacity, block_edge, block_edge...  179 us
    dot_general x4, matrix products, matmul(): jnp.dot(left_side, right_side, preferred_element_type=jnp.float32, precis...  53.3 us
    scatter x1, local copies, waits for them, and re-layouts, local(): outgoing = jnp.zeros((devices * capacity, block_edge, block_edge), jnp.fl...  20.8 us
    scatter-add x1, other arithmetic, local(): jnp.zeros(parent_in.shape, jnp.float32).at[markers]  17 us
    select_n x4, other arithmetic, spread_2(): jnp.where(lax.axis_index(axis) == source, block, jnp.zeros_like(block))  13.9 us
  transfers between devices with their start and end apart: 6, of which 5 were waited for; matrix products, arithmetic and copies ran while one was open for 13% of the time, Pallas kernels for 0%

commit v1 on v0

v1 whole, which is shorter than its diff:
```python
import functools

import jax
import jax.numpy as jnp
from jax import lax
from jax.experimental import pallas as pl
from jax.experimental.pallas import tpu as pltpu
from jax.sharding import PartitionSpec as P

MESH = pl.DeviceIdType.MESH
ANY = pl.BlockSpec(memory_space=pl.ANY)
VMEM = pl.BlockSpec(memory_space=pltpu.VMEM)
SMEM = pl.BlockSpec(memory_space=pltpu.SMEM)


def matmul(left_side, right_side):
    return jnp.dot(
        left_side, right_side, preferred_element_type=jnp.float32, precision=lax.Precision.HIGH
    )


def chip_paths(chips):
    order = [i ^ (i >> 1) for i in range(chips)]
    if sorted(order) != list(range(chips)):
        order = list(range(chips))
    return order, [order[0]] + order[1:][::-1]


def pick(value, pairs, default):
    out = jnp.int32(default)
    for key, result in pairs:
        out = jnp.where(value == key, jnp.int32(result), out)
    return out


def spread_kernel(
    nrow, ncol, steps, cols_in, rows_in, cols_out, rows_out,
    row_send, row_recv, half_recv, chain_send, side_send, local_sem,
):
    row = lax.axis_index("row")
    col = lax.axis_index("col")
    chips = ncol // 2
    chip = col // 2
    core = col % 2
    paths = chip_paths(chips)
    half = cols_in.shape[0] // 2
    ch = half // steps
    rh = rows_in.shape[0] // steps
    nexts = [pick(chip, list(zip(p[:-1], p[1:])), 0) for p in paths]
    last = [p[-1] for p in paths]
    next_chip = jnp.where(core == 0, nexts[0], nexts[1])
    is_last = jnp.where(core == 0, chip == last[0], chip == last[1])

    def row_copy(src, k):
        s = pl.ds(k * rh, rh)
        return pltpu.make_async_remote_copy(
            src_ref=src.at[s, :], dst_ref=rows_out.at[s, :],
            send_sem=row_send.at[k], recv_sem=row_recv.at[k],
            device_id=(row + 1, col), device_id_type=MESH,
        )

    def col_copy(src, h, k, send, target):
        s = pl.ds(h * half + k * ch, ch)
        return pltpu.make_async_remote_copy(
            src_ref=src.at[s, :], dst_ref=cols_out.at[s, :],
            send_sem=send, recv_sem=half_recv.at[h, k],
            device_id=(row, target), device_id_type=MESH,
        )

    local_cols = pltpu.make_async_copy(cols_in, cols_out, local_sem.at[0])
    local_rows = pltpu.make_async_copy(rows_in, rows_out, local_sem.at[1])

    @pl.when(row == 0)
    def _():
        local_rows.start()

    @pl.when(col == 0)
    def _():
        local_cols.start()

    def step(k, carry):
        if nrow > 1:
            @pl.when(row == 0)
            def _():
                row_copy(rows_in, k).start()

            @pl.when(row > 0)
            def _():
                row_copy(rows_out, k).wait_recv()

            @pl.when((row > 0) & (row < nrow - 1))
            def _():
                row_copy(rows_out, k).start()

        @pl.when(col == 0)
        def _():
            if chips > 1:
                for h in range(2):
                    col_copy(cols_in, h, k, chain_send.at[h, k], paths[h][1] * 2 + h).start()
            for h in range(2):
                col_copy(cols_in, h, k, side_send.at[h, k], 1).start()

        @pl.when(chip > 0)
        def _():
            col_copy(cols_out, core, k, chain_send.at[core, k], 0).wait_recv()
            col_copy(cols_out, core, k, side_send.at[core, k], chip * 2 + 1 - core).start()

            @pl.when(jnp.logical_not(is_last))
            def _():
                col_copy(
                    cols_out, core, k, chain_send.at[core, k], next_chip * 2 + core
                ).start()

        return carry

    lax.fori_loop(0, steps, step, 0)

    def drain(k, carry):
        if nrow > 1:
            @pl.when(row < nrow - 1)
            def _():
                row_copy(rows_out, k).wait_send()

        @pl.when(col == 0)
        def _():
            for h in range(2):
                if chips > 1:
                    col_copy(cols_in, h, k, chain_send.at[h, k], 1).wait_send()
                col_copy(cols_in, h, k, side_send.at[h, k], 1).wait_send()

        @pl.when(col == 1)
        def _():
            for h in range(2):
                col_copy(cols_out, h, k, chain_send.at[h, k], 0).wait_recv()

        @pl.when(chip > 0)
        def _():
            col_copy(cols_out, 1 - core, k, chain_send.at[core, k], 0).wait_recv()
            col_copy(cols_out, core, k, side_send.at[core, k], 0).wait_send()

            @pl.when(jnp.logical_not(is_last))
            def _():
                col_copy(cols_out, core, k, chain_send.at[core, k], 0).wait_send()

        return carry

    lax.fori_loop(0, steps, drain, 0)

    @pl.when(row == 0)
    def _():
        local_rows.wait()

    @pl.when(col == 0)
    def _():
        local_cols.wait()


def spread(columns, rows, steps=32):
    nrow, ncol = lax.axis_size("row"), lax.axis_size("col")
    dma = pltpu.SemaphoreType.DMA
    return pl.pallas_call(
        functools.partial(spread_kernel, nrow, ncol, steps),
        out_shape=(
            jax.ShapeDtypeStruct(columns.shape, columns.dtype),
            jax.ShapeDtypeStruct(rows.shape, rows.dtype),
        ),
        in_specs=[ANY, ANY],
        out_specs=(VMEM, VMEM),
        scratch_shapes=[
            dma((steps,)), dma((steps,)), dma((2, steps)),
            dma((2, steps)), dma((2, steps)), dma((2,)),
        ],
        compiler_params=pltpu.CompilerParams(has_side_effects=True),
        name="spread",
    )(columns, rows)


def gather_kernel(count, bcols, where, updated, out, sem):
    edge = out.shape[1]

    def step(s, carry):
        b = where[s]
        src = updated.at[
            pl.ds(pl.multiple_of(b // bcols * edge, edge), edge),
            pl.ds(pl.multiple_of(b % bcols * edge, edge), edge),
        ]
        pltpu.make_async_copy(src, out.at[s], sem).start()
        return carry

    lax.fori_loop(0, count, step, 0)
    pltpu.make_async_copy(out, out, sem).wait()


def gather_blocks(where, updated, bcols, edge):
    count = where.shape[0]
    return pl.pallas_call(
        functools.partial(gather_kernel, count, bcols),
        out_shape=jax.ShapeDtypeStruct((count, edge, edge), updated.dtype),
        in_specs=[SMEM, ANY],
        out_specs=VMEM,
        scratch_shapes=[pltpu.SemaphoreType.DMA],
        name="gather_blocks",
    )(where, updated)


def exchange_kernel(
    nrow, ncol, brows, bcols, cap, blocks, labels, arrived, marks,
    send, recv, label_send, label_recv, local_sem,
):
    row = lax.axis_index("row")
    col = lax.axis_index("col")
    n = nrow * ncol
    me = row * ncol + col

    def active(r, c):
        return r * brows + brows - 1 >= c * bcols

    def block_copy(src, target):
        return pltpu.make_async_remote_copy(
            src_ref=blocks.at[pl.ds(target * cap, cap)], dst_ref=arrived.at[pl.ds(src * cap, cap)],
            send_sem=send.at[target], recv_sem=recv.at[src],
            device_id=(target // ncol, target % ncol), device_id_type=MESH,
        )

    def label_copy(src, target):
        return pltpu.make_async_remote_copy(
            src_ref=labels.at[target], dst_ref=marks.at[src],
            send_sem=label_send.at[target], recv_sem=label_recv.at[src],
            device_id=(target // ncol, target % ncol), device_id_type=MESH,
        )

    own_blocks = pltpu.make_async_copy(
        blocks.at[pl.ds(me * cap, cap)], arrived.at[pl.ds(me * cap, cap)], local_sem.at[0]
    )
    own_labels = pltpu.make_async_copy(labels.at[me], marks.at[me], local_sem.at[1])

    @pl.when(active(row, col))
    def _():
        def step(d, carry):
            target = (row + nrow - d % nrow) % nrow * ncol + (col + d // nrow) % ncol
            label_copy(me, target).start()
            block_copy(me, target).start()
            return carry

        lax.fori_loop(1, n, step, 0)
        own_blocks.start()
        own_labels.start()

    def arrive(s, carry):
        @pl.when((s != me) & active(s // ncol, s % ncol))
        def _():
            label_copy(s, 0).wait_recv()
            block_copy(s, 0).wait_recv()

        return carry

    lax.fori_loop(0, n, arrive, 0)

    @pl.when(active(row, col))
    def _():
        def drain(d, carry):
            target = (row + nrow - d % nrow) % nrow * ncol + (col + d // nrow) % ncol
            label_copy(me, target).wait_send()
            block_copy(me, target).wait_send()
            return carry

        lax.fori_loop(1, n, drain, 0)
        own_blocks.wait()
        own_labels.wait()


def exchange(blocks, labels, brows, bcols, cap):
    nrow, ncol = lax.axis_size("row"), lax.axis_size("col")
    n = nrow * ncol
    dma = pltpu.SemaphoreType.DMA
    return pl.pallas_call(
        functools.partial(exchange_kernel, nrow, ncol, brows, bcols, cap),
        out_shape=(
            jax.ShapeDtypeStruct(blocks.shape, blocks.dtype),
            jax.ShapeDtypeStruct(labels.shape, labels.dtype),
        ),
        in_specs=[VMEM, VMEM],
        out_specs=(VMEM, VMEM),
        scratch_shapes=[dma((n,)), dma((n,)), dma((n,)), dma((n,)), dma((2,))],
        compiler_params=pltpu.CompilerParams(has_side_effects=True),
        name="exchange",
    )(blocks, labels)


def add_kernel(per, marks, parent, arrived, out):
    g = pl.program_id(0)

    @pl.when(g == 0)
    def _():
        out[...] = parent[...]

    def step(i, carry):
        m = marks[g * per + i]

        @pl.when(m >= 0)
        def _():
            out[m] = out[m] + arrived[i]

        return carry

    lax.fori_loop(0, per, step, 0)


def add_blocks(marks, parent, arrived):
    count, edge, _ = arrived.shape
    per = count // 8 if count % 8 == 0 else count
    whole = pl.BlockSpec(parent.shape, lambda g: (0, 0, 0))
    return pl.pallas_call(
        functools.partial(add_kernel, per),
        grid=(count // per,),
        out_shape=jax.ShapeDtypeStruct(parent.shape, parent.dtype),
        in_specs=[SMEM, whole, pl.BlockSpec((per, edge, edge), lambda g: (g, 0, 0))],
        out_specs=whole,
        name="add_blocks",
    )(marks, parent, arrived)


def local(front, inverses, block_owner, block_slot, parent_in):
    width = inverses.shape[1]
    nrow, ncol = lax.axis_size("row"), lax.axis_size("col")
    devices = nrow * ncol
    row, col = lax.axis_index("row"), lax.axis_index("col")
    brows, bcols = block_owner.shape
    edge = parent_in.shape[1]
    count = brows * bcols
    cap = max(1, (count + devices - 1) // devices)

    owners = block_owner.reshape(1, count)
    slots = block_slot.reshape(1, 1, count)
    hit = owners == jnp.arange(devices, dtype=jnp.int32)[:, None]
    before = jnp.arange(count)[:, None] < jnp.arange(count)[None, :]
    rank = jnp.dot(
        hit.astype(jnp.float32), before.astype(jnp.float32), preferred_element_type=jnp.float32
    ).astype(jnp.int32)
    chosen = hit[:, None, :] & (rank[:, None, :] == jnp.arange(cap, dtype=jnp.int32)[:, None])
    position = jnp.arange(count, dtype=jnp.int32)
    where = jnp.sum(jnp.where(chosen, position, 0), axis=2).reshape(devices * cap)
    label = jnp.sum(jnp.where(chosen, slots + 1, 0), axis=2) - 1
    labels = jnp.broadcast_to(
        jnp.pad(label, ((0, 0), (0, 128 - cap)), constant_values=-1)[:, None, :], (devices, 8, 128)
    )

    factor_one, rows_one = spread(matmul(front[:, 0:width], inverses[0]), front[0:width, :])
    partial_value = front - matmul(factor_one, rows_one)
    factor_two, rows_two = spread(
        matmul(partial_value[:, width : 2 * width], inverses[1]),
        partial_value[width : 2 * width, :],
    )
    updated = partial_value - matmul(factor_two, rows_two)
    piece = front.shape[0] // ncol
    panels = jnp.concatenate(
        [
            lax.dynamic_slice_in_dim(factor_one, col * piece, piece, 0),
            lax.dynamic_slice_in_dim(factor_two, col * piece, piece, 0),
        ],
        axis=1,
    )

    blocks = gather_blocks(where, updated, bcols, edge)
    arrived, marks = exchange(blocks, labels, brows, bcols, cap)
    sources = jnp.arange(devices, dtype=jnp.int32)
    sends = sources // ncol * brows + brows - 1 >= sources % ncol * bcols
    marks = jnp.where(sends[:, None], marks[:, 0, :cap], -1).reshape(devices * cap)
    parent_out = add_blocks(marks, parent_in, arrived)
    return (updated, panels, parent_out)


def solution(mesh):
    in_specs = (
        P("row", "col"),
        P(),
        P("row", "col"),
        P("row", "col"),
        P(("row", "col"), None, None),
    )
    out_specs = (P("row", "col"), P(("row", "col"), None), P(("row", "col"), None, None))
    return jax.shard_map(local, mesh=mesh, in_specs=in_specs, out_specs=out_specs, check_vma=False)
```

time: 645 us -> 425 us (0.66)
  waiting for transfers between devices: 485 us -> 0 us
  Pallas kernels: 0 us -> 368 us
  local copies, waits for them, and re-layouts: 43.6 us -> 12.2 us
  other arithmetic: 33.6 us -> 2.7 us
  matrix products: 53.3 us -> 39.1 us
  between operations: 14 us -> 0.73 us
  starting transfers between devices: 11.5 us -> 0 us
    pallas_call x0 -> x5, Pallas kernels: none -> 368 us  [the longest x1 208 us: exchange(): pl.pallas_call(functools.partial(exchange_kernel, nrow, ncol, brows, bcol...]
    psum x4 -> x0, waiting for transfers between devices: 306 us -> none  [spread_2(): return lax.psum(block, axis)]
    all_to_all x2 -> x0, waiting for transfers between devices: 179 us -> none  [the longest x1 179 us: local(): lax.all_to_all(outgoing.reshape(devices, capacity, block_edge, block_edge...]
    scatter x2 -> x0, local copies, waits for them, and re-layouts: 21.8 us -> none  [the longest x1 20.8 us: local(): outgoing = jnp.zeros((devices * capacity, block_edge, block_edge), jnp.fl...]
    scatter-add x1 -> x0, other arithmetic: 17 us -> none  [local(): jnp.zeros(parent_in.shape, jnp.float32).at[markers]]
    dot_general x4, matrix products: 53.3 us -> 39 us  [matmul(): jnp.dot(left_side, right_side, preferred_element_type=jnp.float32, precis...]
    select_n x6 -> x1, other arithmetic: 13.9 us -> 0.6 us  [local(): jnp.where(sends[:, None], marks[:, 0, :cap], -1).reshape(devices * cap)]
    all_to_all x2 -> x0, starting transfers between devices: 11.3 us -> none  [the longest x1 6.78 us: local(): lax.all_to_all(outgoing.reshape(devices, capacity, block_edge, block_edge...]
  transfers between devices with their start and end apart: 6 -> 0, of which waited for: 5 -> 0; matrix products, arithmetic and copies ran while one was open for 13% -> 0% of each run, Pallas kernels for 0% -> 0%
where the time goes in v1:
time: 425 us; the launch traced here: 423 us
  Pallas kernels  368 us (87%)
  matrix products  39.1 us (9%)
  local copies, waits for them, and re-layouts  12.2 us (3%)
    pallas_call x1, Pallas kernels, exchange(): pl.pallas_call(functools.partial(exchange_kernel, nrow, ncol, brows, bcol...  208 us
    pallas_call x2, Pallas kernels, spread(): pl.pallas_call(functools.partial(spread_kernel, nrow, ncol, steps), out_s...  132 us
    dot_general x4, matrix products, matmul(): jnp.dot(left_side, right_side, preferred_element_type=jnp.float32, precis...  39 us
    pallas_call x1, Pallas kernels, gather_blocks(): pl.pallas_call(functools.partial(gather_kernel, count, bcols), out_shape=...  18.5 us
    pallas_call x1, Pallas kernels, add_blocks(): pl.pallas_call(functools.partial(add_kernel, per), grid=(count // per,),...  9.46 us

profile of v1, /device:TPU:7, one launch (start us, length us, event | category | flops | bytes accessed | tf_op | source)
XLA Modules:
  0.0 422.6 jit_solution(6146370057587762581)
XLA Ops:
  0.6 0.0 copy-start.1
  0.7 0.1 broadcast_in_dim.44
  0.7 0.1 broadcast_in_dim.45
  0.8 0.8 broadcast_add_fusion
  1.7 0.1 copy.14
  1.7 0.1 add.49
  1.8 0.8 copy.12
  2.6 0.1 eq.34
  2.7 0.1 convolution_convert_fusion
  2.8 0.2 select_reduce_fusion
  3.1 0.1 copy.16
  3.1 0.1 copy.13
  3.2 0.7 reshape.69.where
  3.9 0.6 broadcast_in_dim.49.labels
  4.6 3.2 slice.23.rows_in
  7.7 0.0 copy-done.1
  7.7 7.1 %fusion.2.cols_in = f32[2048,512]{1,0:T(8,128)} fusion(f32[2048,1024]{1,0:T(8,128)} %param.5, f32[2,512,512]{2,1,0:T(8,128)S(1)} %copy-done.1), kind=kOutput, calls=%fused_computation.2 | convolution fusion | flops 3221225472 | bytes 9437184 | tf_op jit(solution)/shard_map/dot_general | solution.py:17
  14.9 58.7 %spread.2 = (f32[2048,512]{1,0:T(8,128)}, f32[512,1024]{1,0:T(8,128)}) custom-call(f32[2048,512]{1,0:T(8,128)} %fusion.2.cols_in, f32[512,1024]{1,0:T(8,128)} %slice.23.rows_in), custom_call_target="tpu_custom_call" | custom-call | tf_op jit(solution)/shard_map/spread/pallas_call | solution.py:161
  73.6 14.2 %convolution_subtract_fusion.1 = f32[2048,1024]{1,0:T(8,128)S(1)} fusion(f32[2048,1024]{1,0:T(8,128)} %param.5, f32[2048,512]{1,0:T(8,128)} %get-tuple-element.9, f32[512,1024]{1,0:T(8,128)} %get-tuple-element.10), kind=kOutput, calls=%fused_computation.5 | convolution fusion | flops 6444548096 | bytes 23068672 | tf_op jit(solution)/shard_map/dot_general | solution.py:17
  87.8 0.0 copy-start
  87.8 1.6 slice.29.rows_in
  89.4 2.4 copy-done
  91.8 4.9 %fusion.cols_in = f32[2048,512]{1,0:T(8,128)} fusion(f32[2048,1024]{1,0:T(8,128)S(1)} %convolution_subtract_fusion.1, f32[2,512,512]{2,1,0:T(8,128)S(1)} %copy-done.1), kind=kOutput, calls=%fused_computation | convolution fusion | flops 3221225472 | bytes 9437184 | tf_op jit(solution)/shard_map/dot_general | solution.py:17
  96.7 73.1 %spread.3 = (f32[2048,512]{1,0:T(8,128)}, f32[512,1024]{1,0:T(8,128)}) custom-call(f32[2048,512]{1,0:T(8,128)} %fusion.cols_in, f32[512,1024]{1,0:T(8,128)} %slice.29.rows_in), custom_call_target="tpu_custom_call" | custom-call | tf_op jit(solution)/shard_map/spread/pallas_call | solution.py:161
  169.8 1.3 constant_dynamic-slice_fusion
  171.1 12.7 %convolution_subtract_fusion.updated = f32[2048,1024]{1,0:T(8,128)} fusion(f32[2048,1024]{1,0:T(8,128)} %copy-done, f32[2048,512]{1,0:T(8,128)} %get-tuple-element.11, f32[512,1024]{1,0:T(8,128)} %get-tuple-element.12), kind=kOutput, calls=%fused_computation.4 | convolution fusion | flops 6444548096 | bytes 23068672 | tf_op jit(solution)/shard_map/dot_general | solution.py:17
  183.8 1.1 pad_maximum_fusion
  184.9 18.5 %gather_blocks.1.blocks = f32[128,128,128]{2,1,0:T(8,128)} custom-call(s32[128]{0:T(128)} %reshape.69.where, f32[2048,1024]{1,0:T(8,128)} %convolution_subtract_fusion.updated), custom_call_target="tpu_custom_call" | custom-call | tf_op jit(solution)/shard_map/gather_blocks/pallas_call | solution.py:196
  203.4 208.1 %exchange.1 = (f32[128,128,128]{2,1,0:T(8,128)}, s32[32,8,128]{2,1,0:T(8,128)}) custom-call(f32[128,128,128]{2,1,0:T(8,128)} %gather_blocks.1.blocks, s32[32,8,128]{2,1,0:T(8,128)} %broadcast_in_dim.49.labels), custom_call_target="tpu_custom_call" | custom-call | tf_op jit(solution)/shard_map/exchange/pallas_call | solution.py:276
  411.5 0.9 slice_reduce_fusion
  412.5 0.1 squeeze.11
  412.6 0.6 broadcast_select_fusion.marks
  413.2 9.5 %add_blocks.1 = f32[48,128,128]{2,1,0:T(8,128)} custom-call(s32[128]{0:T(128)} %broadcast_select_fusion.marks, f32[48,128,128]{2,1,0:T(8,128)} %parent.1, f32[128,128,128]{2,1,0:T(8,128)} %get-tuple-element.14.arrived), custom_call_target="tpu_custom_call" | custom-call | tf_op jit(solution)/shard_map/add_blocks/pallas_call | solution.py:313
  (4 shorter events, 0.0 us)
Async XLA Ops:
  0.6 7.1 %copy-start.1 = (f32[2,512,512]{2,1,0:T(8,128)S(1)}, f32[2,512,512]{2,1,0:T(8,128)}, u32[]{:S(2)}) copy-start(f32[2,512,512]{2,1,0:T(8,128)} %param.6) | copy-start | bytes 6291460
  87.8 4.0 copy-start

commit v2 on v1

--- a/solution.py
+++ b/solution.py
@@ -34,7 +34,7 @@
 
 
 def spread_kernel(
-    nrow, ncol, steps, cols_in, rows_in, cols_out, rows_out,
+    nrow, ncol, width, front, cols_out, rows_out, corner_out,
     row_send, row_recv, half_recv, chain_send, side_send, local_sem,
 ):
     row = lax.axis_index("row")
@@ -43,19 +43,23 @@
     chip = col // 2
     core = col % 2
     paths = chip_paths(chips)
-    half = cols_in.shape[0] // 2
+    steps = 32
+    half = cols_out.shape[0] // 2
     ch = half // steps
-    rh = rows_in.shape[0] // steps
+    quarter = steps // 2
+    rh = width // quarter
+    corner = steps // 4
+    kh = width // 2 // corner
     nexts = [pick(chip, list(zip(p[:-1], p[1:])), 0) for p in paths]
-    last = [p[-1] for p in paths]
     next_chip = jnp.where(core == 0, nexts[0], nexts[1])
-    is_last = jnp.where(core == 0, chip == last[0], chip == last[1])
-
-    def row_copy(src, k):
-        s = pl.ds(k * rh, rh)
-        return pltpu.make_async_remote_copy(
-            src_ref=src.at[s, :], dst_ref=rows_out.at[s, :],
-            send_sem=row_send.at[k], recv_sem=row_recv.at[k],
+    is_last = jnp.where(core == 0, chip == paths[0][-1], chip == paths[1][-1])
+    pieces = ((1, 0), (0, 1), (0, 0), (1, 1))
+
+    def row_copy(src, q, k):
+        s = (pl.ds(pieces[q][0] * width + k * rh, rh), pl.ds(pieces[q][1] * width, width))
+        return pltpu.make_async_remote_copy(
+            src_ref=src.at[s], dst_ref=rows_out.at[s],
+            send_sem=row_send.at[q * quarter + k], recv_sem=row_recv.at[q * quarter + k],
             device_id=(row + 1, col), device_id_type=MESH,
         )
 
@@ -63,88 +67,175 @@
         s = pl.ds(h * half + k * ch, ch)
         return pltpu.make_async_remote_copy(
             src_ref=src.at[s, :], dst_ref=cols_out.at[s, :],
-            send_sem=send, recv_sem=half_recv.at[h, k],
+            send_sem=send.at[h, k], recv_sem=half_recv.at[h, k],
             device_id=(row, target), device_id_type=MESH,
         )
 
-    local_cols = pltpu.make_async_copy(cols_in, cols_out, local_sem.at[0])
-    local_rows = pltpu.make_async_copy(rows_in, rows_out, local_sem.at[1])
+    def corner_copy(src, first, h, k, i, send, target):
+        at = h * (width // 2) + k * kh
+        to = corner_out.at[i, pl.ds(at, kh), :]
+        if first:
+            src = src.at[pl.ds(pieces[i][0] * width + at, kh), pl.ds(pieces[i][1] * width, width)]
+        else:
+            src = to
+        slot = steps + i * corner + k
+        return pltpu.make_async_remote_copy(
+            src_ref=src, dst_ref=to,
+            send_sem=send.at[h, slot], recv_sem=half_recv.at[h, slot],
+            device_id=(row, target), device_id_type=MESH,
+        )
+
+    local_cols = pltpu.make_async_copy(front, cols_out, local_sem.at[0])
+    local_rows = pltpu.make_async_copy(
+        front.at[pl.ds(0, 2 * width), :], rows_out, local_sem.at[1]
+    )
+
+    def local_corner(src, i):
+        return pltpu.make_async_copy(
+            src.at[pl.ds(pieces[i][0] * width, width), pl.ds(pieces[i][1] * width, width)],
+            corner_out.at[i], local_sem.at[2 + i],
+        )
+
+    def source_sends(h, make):
+        if chips > 1:
+            make(h, chain_send, paths[h][1] * 2 + h).start()
+        make(h, side_send, 1).start()
 
     @pl.when(row == 0)
     def _():
+        if nrow > 1:
+            for q in range(4):
+                def first(k, carry, q=q):
+                    row_copy(front, q, k).start()
+                    return carry
+
+                lax.fori_loop(0, quarter, first, 0)
         local_rows.start()
 
     @pl.when(col == 0)
     def _():
+        def first(k, carry):
+            for h in range(2):
+                source_sends(h, lambda h, send, to: col_copy(front, h, k, send, to))
+            return carry
+
+        lax.fori_loop(0, steps, first, 0)
         local_cols.start()
 
-    def step(k, carry):
+    def pass_rows(q, k):
         if nrow > 1:
-            @pl.when(row == 0)
-            def _():
-                row_copy(rows_in, k).start()
-
             @pl.when(row > 0)
             def _():
-                row_copy(rows_out, k).wait_recv()
+                row_copy(rows_out, q, k).wait_recv()
 
             @pl.when((row > 0) & (row < nrow - 1))
             def _():
-                row_copy(rows_out, k).start()
-
-        @pl.when(col == 0)
-        def _():
-            if chips > 1:
-                for h in range(2):
-                    col_copy(cols_in, h, k, chain_send.at[h, k], paths[h][1] * 2 + h).start()
-            for h in range(2):
-                col_copy(cols_in, h, k, side_send.at[h, k], 1).start()
-
+                row_copy(rows_out, q, k).start()
+
+    def pass_columns(make):
         @pl.when(chip > 0)
         def _():
-            col_copy(cols_out, core, k, chain_send.at[core, k], 0).wait_recv()
-            col_copy(cols_out, core, k, side_send.at[core, k], chip * 2 + 1 - core).start()
+            make(core, chain_send, 0).wait_recv()
+            make(core, side_send, chip * 2 + 1 - core).start()
 
             @pl.when(jnp.logical_not(is_last))
             def _():
-                col_copy(
-                    cols_out, core, k, chain_send.at[core, k], next_chip * 2 + core
-                ).start()
-
-        return carry
-
-    lax.fori_loop(0, steps, step, 0)
-
-    def drain(k, carry):
-        if nrow > 1:
-            @pl.when(row < nrow - 1)
-            def _():
-                row_copy(rows_out, k).wait_send()
-
+                make(core, chain_send, next_chip * 2 + core).start()
+
+    for q in range(2):
+        def both(k, carry, q=q):
+            pass_rows(q, k)
+            pass_columns(lambda h, send, to: col_copy(cols_out, h, q * quarter + k, send, to))
+            return carry
+
+        lax.fori_loop(0, quarter, both, 0)
+
+    for i in range(2):
+        @pl.when((col == 0) & (row == 0))
+        def _(i=i):
+            local_corner(front, i).start()
+
+            def give(k, carry):
+                for h in range(2):
+                    source_sends(
+                        h, lambda h, send, to: corner_copy(front, True, h, k, i, send, to)
+                    )
+                return carry
+
+            lax.fori_loop(0, corner, give, 0)
+
+        @pl.when((col == 0) & (row > 0))
+        def _(i=i):
+            local_corner(rows_out, i).start()
+
+            def give(k, carry):
+                for h in range(2):
+                    source_sends(
+                        h, lambda h, send, to: corner_copy(rows_out, True, h, k, i, send, to)
+                    )
+                return carry
+
+            lax.fori_loop(0, corner, give, 0)
+
+    for i in range(2):
+        def third(k, carry, i=i):
+            pass_rows(2, i * corner + k)
+            pass_columns(
+                lambda h, send, to: corner_copy(corner_out, False, h, k, i, send, to)
+            )
+            return carry
+
+        lax.fori_loop(0, corner, third, 0)
+
+    def fourth(k, carry):
+        pass_rows(3, k)
+        return carry
+
+    lax.fori_loop(0, quarter, fourth, 0)
+
+    if nrow > 1:
+        @pl.when(row < nrow - 1)
+        def _():
+            for q in range(4):
+                def sent(k, carry, q=q):
+                    row_copy(rows_out, q, k).wait_send()
+                    return carry
+
+                lax.fori_loop(0, quarter, sent, 0)
+
+    def drain(make):
         @pl.when(col == 0)
         def _():
             for h in range(2):
                 if chips > 1:
-                    col_copy(cols_in, h, k, chain_send.at[h, k], 1).wait_send()
-                col_copy(cols_in, h, k, side_send.at[h, k], 1).wait_send()
+                    make(h, chain_send).wait_send()
+                make(h, side_send).wait_send()
 
         @pl.when(col == 1)
         def _():
             for h in range(2):
-                col_copy(cols_out, h, k, chain_send.at[h, k], 0).wait_recv()
+                make(h, chain_send).wait_recv()
 
         @pl.when(chip > 0)
         def _():
-            col_copy(cols_out, 1 - core, k, chain_send.at[core, k], 0).wait_recv()
-            col_copy(cols_out, core, k, side_send.at[core, k], 0).wait_send()
+            make(1 - core, chain_send).wait_recv()
+            make(core, side_send).wait_send()
 
             @pl.when(jnp.logical_not(is_last))
             def _():
-                col_copy(cols_out, core, k, chain_send.at[core, k], 0).wait_send()
-
-        return carry
-
-    lax.fori_loop(0, steps, drain, 0)
+                make(core, chain_send).wait_send()
+
+    def drain_columns(k, carry):
+        drain(lambda h, send: col_copy(cols_out, h, k, send, 0))
+        return carry
+
+    lax.fori_loop(0, steps, drain_columns, 0)
+    for i in range(2):
+        def drain_corner(k, carry, i=i):
+            drain(lambda h, send: corner_copy(corner_out, False, h, k, i, send, 0))
+            return carry
+
+        lax.fori_loop(0, corner, drain_corner, 0)
 
     @pl.when(row == 0)
     def _():
@@ -153,26 +244,29 @@
     @pl.when(col == 0)
     def _():
         local_cols.wait()
-
-
-def spread(columns, rows, steps=32):
+        for i in range(2):
+            local_corner(rows_out, i).wait()
+
+
+def spread(front, width):
     nrow, ncol = lax.axis_size("row"), lax.axis_size("col")
     dma = pltpu.SemaphoreType.DMA
+    shape = functools.partial(jax.ShapeDtypeStruct, dtype=front.dtype)
     return pl.pallas_call(
-        functools.partial(spread_kernel, nrow, ncol, steps),
+        functools.partial(spread_kernel, nrow, ncol, width),
         out_shape=(
-            jax.ShapeDtypeStruct(columns.shape, columns.dtype),
-            jax.ShapeDtypeStruct(rows.shape, rows.dtype),
+            shape((front.shape[0], 2 * width)),
+            shape((2 * width, front.shape[1])),
+            shape((2, width, width)),
         ),
-        in_specs=[ANY, ANY],
-        out_specs=(VMEM, VMEM),
+        in_specs=[ANY],
+        out_specs=(VMEM, VMEM, VMEM),
         scratch_shapes=[
-            dma((steps,)), dma((steps,)), dma((2, steps)),
-            dma((2, steps)), dma((2, steps)), dma((2,)),
+            dma((64,)), dma((64,)), dma((2, 48)), dma((2, 48)), dma((2, 48)), dma((4,)),
         ],
         compiler_params=pltpu.CompilerParams(has_side_effects=True),
         name="spread",
-    )(columns, rows)
+    )(front)
 
 
 def gather_kernel(count, bcols, where, updated, out, sem):
@@ -204,8 +298,8 @@
 
 
 def exchange_kernel(
-    nrow, ncol, brows, bcols, cap, blocks, labels, arrived, marks,
-    send, recv, label_send, label_recv, local_sem,
+    nrow, ncol, brows, bcols, cap, blocks, labels, arrived, marks, middle,
+    send, middle_recv, pass_send, recv, label_send, label_recv, local_sem,
 ):
     row = lax.axis_index("row")
     col = lax.axis_index("col")
@@ -215,53 +309,120 @@
     def active(r, c):
         return r * brows + brows - 1 >= c * bcols
 
-    def block_copy(src, target):
-        return pltpu.make_async_remote_copy(
-            src_ref=blocks.at[pl.ds(target * cap, cap)], dst_ref=arrived.at[pl.ds(src * cap, cap)],
-            send_sem=send.at[target], recv_sem=recv.at[src],
+    def piece(index):
+        return pl.ds(index * cap, cap)
+
+    def hop(to_row, to_col):
+        target = to_row * ncol + to_col
+        return pltpu.make_async_remote_copy(
+            src_ref=blocks.at[piece(target)], dst_ref=middle.at[piece(to_row * ncol + col)],
+            send_sem=send.at[target], recv_sem=middle_recv.at[to_row * ncol + col],
+            device_id=(row, to_col), device_id_type=MESH,
+        )
+
+    def relay(to_row, from_col):
+        return pltpu.make_async_remote_copy(
+            src_ref=middle.at[piece(to_row * ncol + from_col)],
+            dst_ref=arrived.at[piece(row * ncol + from_col)],
+            send_sem=pass_send.at[to_row * ncol + from_col],
+            recv_sem=recv.at[row * ncol + from_col],
+            device_id=(to_row, col), device_id_type=MESH,
+        )
+
+    def straight(source, target):
+        return pltpu.make_async_remote_copy(
+            src_ref=blocks.at[piece(target)], dst_ref=arrived.at[piece(source)],
+            send_sem=send.at[target], recv_sem=recv.at[source],
             device_id=(target // ncol, target % ncol), device_id_type=MESH,
         )
 
-    def label_copy(src, target):
-        return pltpu.make_async_remote_copy(
-            src_ref=labels.at[target], dst_ref=marks.at[src],
-            send_sem=label_send.at[target], recv_sem=label_recv.at[src],
+    def label_copy(source, target):
+        return pltpu.make_async_remote_copy(
+            src_ref=labels.at[target], dst_ref=marks.at[source],
+            send_sem=label_send.at[target], recv_sem=label_recv.at[source],
             device_id=(target // ncol, target % ncol), device_id_type=MESH,
         )
 
-    own_blocks = pltpu.make_async_copy(
-        blocks.at[pl.ds(me * cap, cap)], arrived.at[pl.ds(me * cap, cap)], local_sem.at[0]
-    )
+    own_blocks = pltpu.make_async_copy(blocks.at[piece(me)], arrived.at[piece(me)], local_sem.at[0])
     own_labels = pltpu.make_async_copy(labels.at[me], marks.at[me], local_sem.at[1])
 
+    order = [(nrow // 2 + i) % nrow for i in range(nrow)]
+    order = [o for o in order if o != 0]
+
     @pl.when(active(row, col))
     def _():
-        def step(d, carry):
-            target = (row + nrow - d % nrow) % nrow * ncol + (col + d // nrow) % ncol
-            label_copy(me, target).start()
-            block_copy(me, target).start()
-            return carry
-
-        lax.fori_loop(1, n, step, 0)
+        for o in order:
+            straight(me, (row + o) % nrow * ncol + col).start()
+
+        def step(j, carry):
+            to_col = (col + j) % ncol
+            for o in order:
+                hop((row + o) % nrow, to_col).start()
+            return carry
+
+        lax.fori_loop(1, ncol, step, 0)
+
+        def inside(j, carry):
+            straight(me, row * ncol + (col + j) % ncol).start()
+            return carry
+
+        lax.fori_loop(1, ncol, inside, 0)
+
+        def label_step(d, carry):
+            label_copy(me, (me + d) % n).start()
+            return carry
+
+        lax.fori_loop(1, n, label_step, 0)
         own_blocks.start()
         own_labels.start()
 
+    def forward(j, carry):
+        from_col = (col + ncol - j) % ncol
+
+        @pl.when(active(row, from_col))
+        def _():
+            for o in order:
+                to_row = (row + o) % nrow
+                pltpu.make_async_remote_copy(
+                    src_ref=blocks.at[piece(0)],
+                    dst_ref=middle.at[piece(to_row * ncol + from_col)],
+                    send_sem=send.at[0], recv_sem=middle_recv.at[to_row * ncol + from_col],
+                    device_id=(row, from_col), device_id_type=MESH,
+                ).wait_recv()
+                relay(to_row, from_col).start()
+
+        return carry
+
+    lax.fori_loop(1, ncol, forward, 0)
+
     def arrive(s, carry):
         @pl.when((s != me) & active(s // ncol, s % ncol))
         def _():
             label_copy(s, 0).wait_recv()
-            block_copy(s, 0).wait_recv()
+            straight(s, 0).wait_recv()
 
         return carry
 
     lax.fori_loop(0, n, arrive, 0)
 
+    def passed(j, carry):
+        from_col = (col + ncol - j) % ncol
+
+        @pl.when(active(row, from_col))
+        def _():
+            for o in order:
+                relay((row + o) % nrow, from_col).wait_send()
+
+        return carry
+
+    lax.fori_loop(1, ncol, passed, 0)
+
     @pl.when(active(row, col))
     def _():
         def drain(d, carry):
-            target = (row + nrow - d % nrow) % nrow * ncol + (col + d // nrow) % ncol
+            target = (me + d) % n
             label_copy(me, target).wait_send()
-            block_copy(me, target).wait_send()
+            straight(me, target).wait_send()
             return carry
 
         lax.fori_loop(1, n, drain, 0)
@@ -281,7 +442,10 @@
         ),
         in_specs=[VMEM, VMEM],
         out_specs=(VMEM, VMEM),
-        scratch_shapes=[dma((n,)), dma((n,)), dma((n,)), dma((n,)), dma((2,))],
+        scratch_shapes=[
+            pltpu.VMEM(blocks.shape, blocks.dtype),
+            dma((n,)), dma((n,)), dma((n,)), dma((n,)), dma((n,)), dma((n,)), dma((2,)),
+        ],
         compiler_params=pltpu.CompilerParams(has_side_effects=True),
         name="exchange",
     )(blocks, labels)
@@ -345,13 +509,13 @@
         jnp.pad(label, ((0, 0), (0, 128 - cap)), constant_values=-1)[:, None, :], (devices, 8, 128)
     )
 
-    factor_one, rows_one = spread(matmul(front[:, 0:width], inverses[0]), front[0:width, :])
-    partial_value = front - matmul(factor_one, rows_one)
-    factor_two, rows_two = spread(
-        matmul(partial_value[:, width : 2 * width], inverses[1]),
-        partial_value[width : 2 * width, :],
-    )
-    updated = partial_value - matmul(factor_two, rows_two)
+    columns, rows, corner = spread(front, width)
+    below, right = corner[0], corner[1]
+    rows_one = rows[:width]
+    factor_one = matmul(columns[:, :width], inverses[0])
+    factor_two = matmul(columns[:, width:] - matmul(factor_one, right), inverses[1])
+    rows_two = rows[width:] - matmul(matmul(below, inverses[0]), rows_one)
+    updated = front - matmul(factor_one, rows_one) - matmul(factor_two, rows_two)
     piece = front.shape[0] // ncol
     panels = jnp.concatenate(
         [

time: 425 us -> 374 us (0.88)
  Pallas kernels: 368 us -> 320 us
    pallas_call x2 -> x1, Pallas kernels: 132 us -> 106 us  [spread(): pl.pallas_call(functools.partial(spread_kernel, nrow, ncol, width), out_s...]
    pallas_call x1, Pallas kernels: 208 us -> 185 us  [exchange(): pl.pallas_call(functools.partial(exchange_kernel, nrow, ncol, brows, bcol...]
    slice x2 -> x0, local copies, waits for them, and re-layouts: 4.76 us -> none  [the longest x1 3.16 us: local(): front[0:width, :]]
    dot_general x4 -> x7, matrix products: 39 us -> 40.3 us  [matmul(): jnp.dot(left_side, right_side, preferred_element_type=jnp.float32, precis...]
where the time goes in v2:
time: 374 us; the launch traced here: 372 us
  Pallas kernels  320 us (86%)
  matrix products  40.4 us (11%)
  local copies, waits for them, and re-layouts  8.28 us (2%)
    pallas_call x1, Pallas kernels, exchange(): pl.pallas_call(functools.partial(exchange_kernel, nrow, ncol, brows, bcol...  185 us
    pallas_call x1, Pallas kernels, spread(): pl.pallas_call(functools.partial(spread_kernel, nrow, ncol, width), out_s...  106 us
    dot_general x7, matrix products, matmul(): jnp.dot(left_side, right_side, preferred_element_type=jnp.float32, precis...  40.3 us
    pallas_call x1, Pallas kernels, gather_blocks(): pl.pallas_call(functools.partial(gather_kernel, count, bcols), out_shape=...  18.5 us
    pallas_call x1, Pallas kernels, add_blocks(): pl.pallas_call(functools.partial(add_kernel, per), grid=(count // per,),...  9.46 us

profile of v2, /device:TPU:7, one launch (start us, length us, event | category | flops | bytes accessed | tf_op | source)
XLA Modules:
  0.0 371.9 jit_solution(12641849820669080595)
XLA Ops:
  0.6 0.1 broadcast_in_dim.44
  0.7 0.1 broadcast_in_dim.45
  0.8 0.7 broadcast_add_fusion
  1.5 0.1 copy.16
  1.6 0.1 add.49
  1.7 0.8 copy.14
  2.5 0.1 eq.34
  2.6 0.1 convolution_convert_fusion
  2.7 0.2 select_reduce_fusion
  2.9 0.1 copy.19
  3.0 0.1 copy.15
  3.1 0.7 reshape.69.where
  3.8 0.7 broadcast_in_dim.49.labels
  4.5 0.0 copy-start.5
  4.5 106.4 %spread.1 = (f32[2048,1024]{1,0:T(8,128)}, f32[1024,1024]{1,0:T(8,128)}, f32[2,512,512]{2,1,0:T(8,128)}) custom-call(f32[2048,1024]{1,0:T(8,128)} %front.1), custom_call_target="tpu_custom_call" | custom-call | tf_op jit(solution)/shard_map/spread/pallas_call | solution.py:255
  110.8 0.0 copy-start.4
  110.9 0.0 copy-done.5
  110.9 2.4 fusion.11
  113.3 3.7 %fusion.7 = f32[512,1024]{1,0:T(8,128)S(1)} fusion(f32[512,512]{1,0:T(8,128)S(1)} %fusion.11, f32[1024,1024]{1,0:T(8,128)} %get-tuple-element.9), kind=kOutput, calls=%fused_computation.8 | convolution fusion | flops 1610612736 | bytes 5242880 | tf_op jit(solution)/shard_map/dot_general | solution.py:17
  117.0 0.0 copy-done.4
  117.0 0.0 copy-start.7
  117.0 4.9 %fusion.3 = f32[2048,512]{0,1:T(8,128)S(1)} fusion(f32[2048,1024]{1,0:T(8,128)S(1)} %copy-done.4, f32[2,512,512]{2,1,0:T(8,128)} %param.6), kind=kOutput, calls=%fused_computation.4 | convolution fusion | flops 3221225472 | bytes 9437184 | tf_op jit(solution)/shard_map/dot_general | solution.py:17
  121.9 0.0 copy-done.7
  121.9 0.0 copy-start
  121.9 0.0 copy-start.6
  121.9 3.5 fusion.14
  125.4 0.0 copy-done.6
  125.4 3.8 %fusion = f32[2048,512]{0,1:T(8,128)S(1)} fusion(f32[2048,512]{1,0:T(8,128)S(1)} %fusion.14, f32[2048,1024]{1,0:T(8,128)S(1)} %copy-done.4, f32[2,512,512]{2,1,0:T(8,128)S(1)} %copy-done.6), kind=kOutput, calls=%fused_computation.1 | convolution fusion | flops 3222274048 | bytes 13631488 | tf_op jit(solution)/shard_map/dot_general | solution.py:17
  129.2 0.0 copy-done
  129.3 0.0 copy-start.1
  129.3 0.1 constant_dynamic-slice_fusion
  129.4 1.8 copy-done.1
  131.2 1.0 pad_maximum_fusion
  132.2 2.5 copy.18
  134.8 0.0 copy-start.2
  134.8 0.0 copy-start.3
  134.8 9.8 %fusion.9 = f32[2048,1024]{1,0:T(8,128)S(1)} fusion(f32[2048,512]{0,1:T(8,128)} %copy-done, f32[1024,1024]{1,0:T(8,128)} %get-tuple-element.9), kind=kOutput, calls=%fused_computation.10 | convolution fusion | flops 6442450944 | bytes 14680064 | tf_op jit(solution)/shard_map/dot_general | solution.py:17
  144.6 0.0 copy-done.2
  144.6 0.0 copy-done.3
  144.6 12.2 %subtract_subtract_fusion.updated = f32[2048,1024]{1,0:T(8,128)} fusion(f32[2048,1024]{1,0:T(8,128)} %front.1, f32[2048,1024]{1,0:T(8,128)S(1)} %fusion.9, f32[2048,512]{0,1:T(8,128)S(1)} %copy-done.2, f32[512,1024]{1,0:T(8,128)S(1)} %fusion.7, f32[1024,1024]{1,0:T(8,128)S(1)} %copy-done.3), kind=kOutput, calls=%fused_computation | convolution fusion | flops 6447169536 | bytes 33554432 | tf_op jit(solution)/shard_map/dot_general | solution.py:17
  156.8 18.5 %gather_blocks.1.blocks = f32[128,128,128]{2,1,0:T(8,128)} custom-call(s32[128]{0:T(128)} %reshape.69.where, f32[2048,1024]{1,0:T(8,128)} %subtract_subtract_fusion.updated), custom_call_target="tpu_custom_call" | custom-call | tf_op jit(solution)/shard_map/gather_blocks/pallas_call | solution.py:290
  175.3 185.5 %exchange.1 = (f32[128,128,128]{2,1,0:T(8,128)}, s32[32,8,128]{2,1,0:T(8,128)}) custom-call(f32[128,128,128]{2,1,0:T(8,128)} %gather_blocks.1.blocks, s32[32,8,128]{2,1,0:T(8,128)} %broadcast_in_dim.49.labels), custom_call_target="tpu_custom_call" | custom-call | tf_op jit(solution)/shard_map/exchange/pallas_call | solution.py:437
  360.8 0.9 slice_reduce_fusion
  361.8 0.1 squeeze.20
  361.9 0.6 broadcast_select_fusion.marks
  362.4 9.5 %add_blocks.1 = f32[48,128,128]{2,1,0:T(8,128)} custom-call(s32[128]{0:T(128)} %broadcast_select_fusion.marks, f32[48,128,128]{2,1,0:T(8,128)} %parent.1, f32[128,128,128]{2,1,0:T(8,128)} %get-tuple-element.12.arrived), custom_call_target="tpu_custom_call" | custom-call | tf_op jit(solution)/shard_map/add_blocks/pallas_call | solution.py:477
  (4 shorter events, 0.0 us)
Async XLA Ops:
  4.5 106.4 %copy-start.5 = (f32[2,512,512]{2,1,0:T(8,128)S(1)}, f32[2,512,512]{2,1,0:T(8,128)}, u32[]{:S(2)}) copy-start(f32[2,512,512]{2,1,0:T(8,128)} %param.6) | copy-start | bytes 6291460
  110.8 6.2 %copy-start.4 = (f32[2048,1024]{1,0:T(8,128)S(1)}, f32[2048,1024]{1,0:T(8,128)}, u32[]{:S(2)}) copy-start(f32[2048,1024]{1,0:T(8,128)} %get-tuple-element.8) | copy-start | bytes 25165828
  117.0 4.9 %copy-start.7 = (f32[2,512,512]{2,1,0:T(8,128)S(1)}, f32[2,512,512]{2,1,0:T(8,128)}, u32[]{:S(2)}) copy-start(f32[2,512,512]{2,1,0:T(8,128)} %get-tuple-element.10) | copy-start | bytes 6291460
  121.9 7.3 %copy-start = (f32[2048,512]{0,1:T(8,128)}, f32[2048,512]{0,1:T(8,128)S(1)}, u32[]{:S(2)}) copy-start(f32[2048,512]{0,1:T(8,128)S(1)} %fusion.3) | copy-start | bytes 12582916
  121.9 3.5 copy-start.6
  129.3 1.9 copy-start.1
  134.8 9.8 %copy-start.2 = (f32[2048,512]{0,1:T(8,128)S(1)}, f32[2048,512]{0,1:T(8,128)}, u32[]{:S(2)}) copy-start(f32[2048,512]{0,1:T(8,128)} %copy-done.1) | copy-start | bytes 12582916
  134.8 9.8 %copy-start.3 = (f32[1024,1024]{1,0:T(8,128)S(1)}, f32[1024,1024]{1,0:T(8,128)}, u32[]{:S(2)}) copy-start(f32[1024,1024]{1,0:T(8,128)} %get-tuple-element.9) | copy-start | bytes 12582916

commit v3 on v2

--- a/solution.py
+++ b/solution.py
@@ -35,6 +35,7 @@
 
 def spread_kernel(
     nrow, ncol, width, front, cols_out, rows_out, corner_out,
+    stage_cols, stage_rows, stage_corner,
     row_send, row_recv, half_recv, chain_send, side_send, local_sem,
 ):
     row = lax.axis_index("row")
@@ -85,16 +86,19 @@
             device_id=(row, target), device_id_type=MESH,
         )
 
-    local_cols = pltpu.make_async_copy(front, cols_out, local_sem.at[0])
+    local_cols = pltpu.make_async_copy(front, stage_cols, local_sem.at[0])
     local_rows = pltpu.make_async_copy(
-        front.at[pl.ds(0, 2 * width), :], rows_out, local_sem.at[1]
+        front.at[pl.ds(0, 2 * width), :], stage_rows, local_sem.at[1]
     )
 
     def local_corner(src, i):
         return pltpu.make_async_copy(
             src.at[pl.ds(pieces[i][0] * width, width), pl.ds(pieces[i][1] * width, width)],
-            corner_out.at[i], local_sem.at[2 + i],
-        )
+            stage_corner.at[i], local_sem.at[2 + i],
+        )
+
+    def store(stage, out, i):
+        return pltpu.make_async_copy(stage, out, local_sem.at[4 + i])
 
     def source_sends(h, make):
         if chips > 1:
@@ -187,6 +191,19 @@
 
         lax.fori_loop(0, corner, third, 0)
 
+    @pl.when(row == 0)
+    def _():
+        local_rows.wait()
+        store(stage_rows, rows_out, 1).start()
+
+    @pl.when(col == 0)
+    def _():
+        local_cols.wait()
+        store(stage_cols, cols_out, 0).start()
+        for i in range(2):
+            local_corner(rows_out, i).wait()
+        store(stage_corner, corner_out, 2).start()
+
     def fourth(k, carry):
         pass_rows(3, k)
         return carry
@@ -239,13 +256,12 @@
 
     @pl.when(row == 0)
     def _():
-        local_rows.wait()
+        store(stage_rows, rows_out, 1).wait()
 
     @pl.when(col == 0)
     def _():
-        local_cols.wait()
-        for i in range(2):
-            local_corner(rows_out, i).wait()
+        store(stage_cols, cols_out, 0).wait()
+        store(stage_corner, corner_out, 2).wait()
 
 
 def spread(front, width):
@@ -260,9 +276,12 @@
             shape((2, width, width)),
         ),
         in_specs=[ANY],
-        out_specs=(VMEM, VMEM, VMEM),
+        out_specs=(ANY, ANY, ANY),
         scratch_shapes=[
-            dma((64,)), dma((64,)), dma((2, 48)), dma((2, 48)), dma((2, 48)), dma((4,)),
+            pltpu.VMEM((front.shape[0], 2 * width), front.dtype),
+            pltpu.VMEM((2 * width, front.shape[1]), front.dtype),
+            pltpu.VMEM((2, width, width), front.dtype),
+            dma((64,)), dma((64,)), dma((2, 48)), dma((2, 48)), dma((2, 48)), dma((7,)),
         ],
         compiler_params=pltpu.CompilerParams(has_side_effects=True),
         name="spread",
@@ -376,19 +395,37 @@
         own_blocks.start()
         own_labels.start()
 
+    def landed(to_row, from_col):
+        return pltpu.make_async_remote_copy(
+            src_ref=blocks.at[piece(0)],
+            dst_ref=middle.at[piece(to_row * ncol + from_col)],
+            send_sem=send.at[0], recv_sem=middle_recv.at[to_row * ncol + from_col],
+            device_id=(row, from_col), device_id_type=MESH,
+        )
+
     def forward(j, carry):
         from_col = (col + ncol - j) % ncol
-
-        @pl.when(active(row, from_col))
-        def _():
-            for o in order:
-                to_row = (row + o) % nrow
-                pltpu.make_async_remote_copy(
-                    src_ref=blocks.at[piece(0)],
-                    dst_ref=middle.at[piece(to_row * ncol + from_col)],
-                    send_sem=send.at[0], recv_sem=middle_recv.at[to_row * ncol + from_col],
-                    device_id=(row, from_col), device_id_type=MESH,
-                ).wait_recv()
+        previous = (col + ncol - j + 1) % ncol
+        mine = active(row, from_col)
+
+        for o in order:
+            to_row = (row + o) % nrow
+
+            @pl.when(mine & (to_row > row))
+            def _(to_row=to_row):
+                landed(to_row, from_col).wait_recv()
+                relay(to_row, from_col).start()
+
+        @pl.when((row < nrow - 1) & active(row + 1, previous))
+        def _():
+            straight((row + 1) * ncol + previous, 0).wait_recv()
+
+        for o in order:
+            to_row = (row + o) % nrow
+
+            @pl.when(mine & (to_row < row))
+            def _(to_row=to_row):
+                landed(to_row, from_col).wait_recv()
                 relay(to_row, from_col).start()
 
         return carry
@@ -399,7 +436,10 @@
         @pl.when((s != me) & active(s // ncol, s % ncol))
         def _():
             label_copy(s, 0).wait_recv()
-            straight(s, 0).wait_recv()
+
+            @pl.when((s // ncol != row + 1) | (s % ncol == (col + 1) % ncol))
+            def _():
+                straight(s, 0).wait_recv()
 
         return carry
 
@@ -440,8 +480,8 @@
             jax.ShapeDtypeStruct(blocks.shape, blocks.dtype),
             jax.ShapeDtypeStruct(labels.shape, labels.dtype),
         ),
-        in_specs=[VMEM, VMEM],
-        out_specs=(VMEM, VMEM),
+        in_specs=[ANY, VMEM],
+        out_specs=(ANY, VMEM),
         scratch_shapes=[
             pltpu.VMEM(blocks.shape, blocks.dtype),
             dma((n,)), dma((n,)), dma((n,)), dma((n,)), dma((n,)), dma((n,)), dma((2,)),
@@ -451,35 +491,52 @@
     )(blocks, labels)
 
 
-def add_kernel(per, marks, parent, arrived, out):
-    g = pl.program_id(0)
-
-    @pl.when(g == 0)
-    def _():
-        out[...] = parent[...]
-
-    def step(i, carry):
-        m = marks[g * per + i]
-
-        @pl.when(m >= 0)
-        def _():
-            out[m] = out[m] + arrived[i]
-
-        return carry
-
-    lax.fori_loop(0, per, step, 0)
-
-
-def add_blocks(marks, parent, arrived):
-    count, edge, _ = arrived.shape
-    per = count // 8 if count % 8 == 0 else count
-    whole = pl.BlockSpec(parent.shape, lambda g: (0, 0, 0))
+def add_kernel(ncol, brows, bcols, cap, marks, parent, arrived, out, held, sem, parent_sem):
+    n = arrived.shape[0] // cap
+
+    def each(body):
+        def step(s, carry):
+            @pl.when(s // ncol * brows + brows - 1 >= s % ncol * bcols)
+            def _():
+                body(s)
+
+            return carry
+
+        lax.fori_loop(0, n, step, 0)
+
+    def fetch(s):
+        part = pl.ds(s * cap, cap)
+        return pltpu.make_async_copy(arrived.at[part], held.at[part], sem.at[s])
+
+    whole = pltpu.make_async_copy(parent, out, parent_sem)
+    whole.start()
+    each(lambda s: fetch(s).start())
+    whole.wait()
+
+    def add(s):
+        fetch(s).wait()
+        for k in range(cap):
+            m = marks[s * cap + k]
+
+            @pl.when(m >= 0)
+            def _(k=k, m=m):
+                out[m] = out[m] + held[s * cap + k]
+
+    each(add)
+
+
+def add_blocks(marks, parent, arrived, brows, bcols, cap):
+    n = arrived.shape[0] // cap
     return pl.pallas_call(
-        functools.partial(add_kernel, per),
-        grid=(count // per,),
+        functools.partial(add_kernel, lax.axis_size("col"), brows, bcols, cap),
         out_shape=jax.ShapeDtypeStruct(parent.shape, parent.dtype),
-        in_specs=[SMEM, whole, pl.BlockSpec((per, edge, edge), lambda g: (g, 0, 0))],
-        out_specs=whole,
+        in_specs=[SMEM, ANY, ANY],
+        out_specs=VMEM,
+        scratch_shapes=[
+            pltpu.VMEM(arrived.shape, arrived.dtype),
+            pltpu.SemaphoreType.DMA((n,)),
+            pltpu.SemaphoreType.DMA,
+        ],
         name="add_blocks",
     )(marks, parent, arrived)
 
@@ -503,7 +560,10 @@
     ).astype(jnp.int32)
     chosen = hit[:, None, :] & (rank[:, None, :] == jnp.arange(cap, dtype=jnp.int32)[:, None])
     position = jnp.arange(count, dtype=jnp.int32)
-    where = jnp.sum(jnp.where(chosen, position, 0), axis=2).reshape(devices * cap)
+    place = jnp.arange(devices * cap, dtype=jnp.int32).reshape(devices, cap) % count
+    filled = jnp.any(chosen, axis=2)
+    where = jnp.where(filled, jnp.sum(jnp.where(chosen, position, 0), axis=2), place)
+    where = where.reshape(devices * cap)
     label = jnp.sum(jnp.where(chosen, slots + 1, 0), axis=2) - 1
     labels = jnp.broadcast_to(
         jnp.pad(label, ((0, 0), (0, 128 - cap)), constant_values=-1)[:, None, :], (devices, 8, 128)
@@ -530,7 +590,7 @@
     sources = jnp.arange(devices, dtype=jnp.int32)
     sends = sources // ncol * brows + brows - 1 >= sources % ncol * bcols
     marks = jnp.where(sends[:, None], marks[:, 0, :cap], -1).reshape(devices * cap)
-    parent_out = add_blocks(marks, parent_in, arrived)
+    parent_out = add_blocks(marks, parent_in, arrived, brows, bcols, cap)
     return (updated, panels, parent_out)
 
 

time: 374 us -> 358 us (0.957)
  Pallas kernels: 320 us -> 305 us
    pallas_call x1, Pallas kernels: 18.5 us -> 7.58 us  [gather_blocks(): pl.pallas_call(functools.partial(gather_kernel, count, bcols), out_shape=...]
    pallas_call x1, Pallas kernels: 106 us -> 101 us  [spread(): pl.pallas_call(functools.partial(spread_kernel, nrow, ncol, width), out_s...]
    pallas_call x1, Pallas kernels: 185 us -> 191 us  [exchange(): pl.pallas_call(functools.partial(exchange_kernel, nrow, ncol, brows, bcol...]
where the time goes in v3:
time: 358 us
  Pallas kernels  305 us (85%)
  matrix products  40.4 us (11%)
  local copies, waits for them, and re-layouts  8 us (2%)
    pallas_call x1, Pallas kernels, exchange(): pl.pallas_call(functools.partial(exchange_kernel, nrow, ncol, brows, bcol...  191 us
    pallas_call x1, Pallas kernels, spread(): pl.pallas_call(functools.partial(spread_kernel, nrow, ncol, width), out_s...  101 us
    dot_general x7, matrix products, matmul(): jnp.dot(left_side, right_side, preferred_element_type=jnp.float32, precis...  40.3 us
    pallas_call x1, Pallas kernels, gather_blocks(): pl.pallas_call(functools.partial(gather_kernel, count, bcols), out_shape=...  7.58 us

profile of v3, /device:TPU:7, one launch (start us, length us, event | category | flops | bytes accessed | tf_op | source)
XLA Modules:
  0.0 358.2 jit_solution(16388819912158471795)
XLA Ops:
  0.6 0.1 broadcast_in_dim.44
  0.7 0.1 broadcast_in_dim.45
  0.8 0.7 broadcast_add_fusion
  1.5 0.1 copy.17
  1.6 0.1 add.60
  1.7 0.8 copy.14
  2.5 0.1 eq.36
  2.6 0.1 convolution_convert_fusion
  2.7 0.2 fusion.24
  2.8 0.2 select_reduce_fusion
  3.1 0.1 copy.15
  3.2 0.1 reduce_or.12
  3.3 0.1 copy.20
  3.4 0.1 copy.16
  3.5 0.1 reduce_sum.21
  3.6 0.1 reshape.86
  3.7 0.6 fusion.25.where
  4.3 0.7 broadcast_in_dim.49.labels
  5.0 0.0 copy-start.5
  5.0 101.2 %spread.1 = (f32[2048,1024]{1,0:T(8,128)}, f32[1024,1024]{1,0:T(8,128)}, f32[2,512,512]{2,1,0:T(8,128)}) custom-call(f32[2048,1024]{1,0:T(8,128)} %front.1), custom_call_target="tpu_custom_call" | custom-call | tf_op jit(solution)/shard_map/spread/pallas_call | solution.py:271
  106.2 0.0 copy-start.4
  106.2 0.0 copy-done.5
  106.2 2.4 fusion.11
  108.6 3.7 %fusion.7 = f32[512,1024]{1,0:T(8,128)S(1)} fusion(f32[512,512]{1,0:T(8,128)S(1)} %fusion.11, f32[1024,1024]{1,0:T(8,128)} %get-tuple-element.9), kind=kOutput, calls=%fused_computation.8 | convolution fusion | flops 1610612736 | bytes 5242880 | tf_op jit(solution)/shard_map/dot_general | solution.py:17
  112.4 0.0 copy-done.4
  112.4 0.0 copy-start.7
  112.4 4.9 %fusion.3 = f32[2048,512]{0,1:T(8,128)S(1)} fusion(f32[2048,1024]{1,0:T(8,128)S(1)} %copy-done.4, f32[2,512,512]{2,1,0:T(8,128)} %param.6), kind=kOutput, calls=%fused_computation.4 | convolution fusion | flops 3221225472 | bytes 9437184 | tf_op jit(solution)/shard_map/dot_general | solution.py:17
  117.3 0.0 copy-done.7
  117.3 0.0 copy-start
  117.3 0.0 copy-start.6
  117.3 3.5 fusion.14
  120.8 0.0 copy-done.6
  120.8 3.8 %fusion = f32[2048,512]{0,1:T(8,128)S(1)} fusion(f32[2048,512]{1,0:T(8,128)S(1)} %fusion.14, f32[2048,1024]{1,0:T(8,128)S(1)} %copy-done.4, f32[2,512,512]{2,1,0:T(8,128)S(1)} %copy-done.6), kind=kOutput, calls=%fused_computation.1 | convolution fusion | flops 3222274048 | bytes 13631488 | tf_op jit(solution)/shard_map/dot_general | solution.py:17
  124.6 0.0 copy-done
  124.6 0.0 copy-start.1
  124.7 0.1 constant_dynamic-slice_fusion
  124.8 1.8 copy-done.1
  126.6 1.0 pad_maximum_fusion
  127.6 2.5 copy.19
  130.2 0.0 copy-start.2
  130.2 0.0 copy-start.3
  130.2 9.8 %fusion.9 = f32[2048,1024]{1,0:T(8,128)S(1)} fusion(f32[2048,512]{0,1:T(8,128)} %copy-done, f32[1024,1024]{1,0:T(8,128)} %get-tuple-element.9), kind=kOutput, calls=%fused_computation.10 | convolution fusion | flops 6442450944 | bytes 14680064 | tf_op jit(solution)/shard_map/dot_general | solution.py:17
  140.0 0.0 copy-done.2
  140.0 0.0 copy-done.3
  140.0 12.2 %subtract_subtract_fusion.updated = f32[2048,1024]{1,0:T(8,128)} fusion(f32[2048,1024]{1,0:T(8,128)} %front.1, f32[2048,1024]{1,0:T(8,128)S(1)} %fusion.9, f32[2048,512]{0,1:T(8,128)S(1)} %copy-done.2, f32[512,1024]{1,0:T(8,128)S(1)} %fusion.7, f32[1024,1024]{1,0:T(8,128)S(1)} %copy-done.3), kind=kOutput, calls=%fused_computation | convolution fusion | flops 6447169536 | bytes 33554432 | tf_op jit(solution)/shard_map/dot_general | solution.py:17
  152.2 7.6 %gather_blocks.1.blocks = f32[128,128,128]{2,1,0:T(8,128)} custom-call(s32[128]{0:T(128)} %fusion.25.where, f32[2048,1024]{1,0:T(8,128)} %subtract_subtract_fusion.updated), custom_call_target="tpu_custom_call" | custom-call | tf_op jit(solution)/shard_map/gather_blocks/pallas_call | solution.py:309
  159.8 190.6 %exchange.1 = (f32[128,128,128]{2,1,0:T(8,128)}, s32[32,8,128]{2,1,0:T(8,128)}) custom-call(f32[128,128,128]{2,1,0:T(8,128)} %gather_blocks.1.blocks, s32[32,8,128]{2,1,0:T(8,128)} %broadcast_in_dim.49.labels), custom_call_target="tpu_custom_call" | custom-call | tf_op jit(solution)/shard_map/exchange/pallas_call | solution.py:477
  350.4 0.9 slice_reduce_fusion
  351.3 0.1 squeeze.20
  351.4 0.5 broadcast_select_fusion.marks
  351.9 6.1 %add_blocks.1 = f32[48,128,128]{2,1,0:T(8,128)} custom-call(s32[128]{0:T(128)} %broadcast_select_fusion.marks, f32[48,128,128]{2,1,0:T(8,128)} %parent.1, f32[128,128,128]{2,1,0:T(8,128)} %get-tuple-element.12.arrived), custom_call_target="tpu_custom_call" | custom-call | tf_op jit(solution)/shard_map/add_blocks/pallas_call | solution.py:530
  (5 shorter events, 0.0 us)
Async XLA Ops:
  5.0 101.2 %copy-start.5 = (f32[2,512,512]{2,1,0:T(8,128)S(1)}, f32[2,512,512]{2,1,0:T(8,128)}, u32[]{:S(2)}) copy-start(f32[2,512,512]{2,1,0:T(8,128)} %param.6) | copy-start | bytes 6291460
  106.2 6.2 %copy-start.4 = (f32[2048,1024]{1,0:T(8,128)S(1)}, f32[2048,1024]{1,0:T(8,128)}, u32[]{:S(2)}) copy-start(f32[2048,1024]{1,0:T(8,128)} %get-tuple-element.8) | copy-start | bytes 25165828
  112.4 4.9 %copy-start.7 = (f32[2,512,512]{2,1,0:T(8,128)S(1)}, f32[2,512,512]{2,1,0:T(8,128)}, u32[]{:S(2)}) copy-start(f32[2,512,512]{2,1,0:T(8,128)} %get-tuple-element.10) | copy-start | bytes 6291460
  117.3 7.3 %copy-start = (f32[2048,512]{0,1:T(8,128)}, f32[2048,512]{0,1:T(8,128)S(1)}, u32[]{:S(2)}) copy-start(f32[2048,512]{0,1:T(8,128)S(1)} %fusion.3) | copy-start | bytes 12582916
  117.3 3.5 copy-start.6
  124.6 1.9 copy-start.1
  130.2 9.8 %copy-start.2 = (f32[2048,512]{0,1:T(8,128)S(1)}, f32[2048,512]{0,1:T(8,128)}, u32[]{:S(2)}) copy-start(f32[2048,512]{0,1:T(8,128)} %copy-done.1) | copy-start | bytes 12582916
  130.2 9.8 %copy-start.3 = (f32[1024,1024]{1,0:T(8,128)S(1)}, f32[1024,1024]{1,0:T(8,128)}, u32[]{:S(2)}) copy-start(f32[1024,1024]{1,0:T(8,128)} %get-tuple-element.9) | copy-start | bytes 12582916

commit v4 on v3

--- a/solution.py
+++ b/solution.py
@@ -405,7 +405,6 @@
 
     def forward(j, carry):
         from_col = (col + ncol - j) % ncol
-        previous = (col + ncol - j + 1) % ncol
         mine = active(row, from_col)
 
         for o in order:
@@ -416,10 +415,6 @@
                 landed(to_row, from_col).wait_recv()
                 relay(to_row, from_col).start()
 
-        @pl.when((row < nrow - 1) & active(row + 1, previous))
-        def _():
-            straight((row + 1) * ncol + previous, 0).wait_recv()
-
         for o in order:
             to_row = (row + o) % nrow
 
@@ -436,10 +431,7 @@
         @pl.when((s != me) & active(s // ncol, s % ncol))
         def _():
             label_copy(s, 0).wait_recv()
-
-            @pl.when((s // ncol != row + 1) | (s % ncol == (col + 1) % ncol))
-            def _():
-                straight(s, 0).wait_recv()
+            straight(s, 0).wait_recv()
 
         return carry
 

time: 358 us -> 357 us (level)
    pallas_call x1, Pallas kernels: 191 us -> 187 us  [exchange(): pl.pallas_call(functools.partial(exchange_kernel, nrow, ncol, brows, bcol...]
where the time goes in v4:
time: 357 us; the launch traced here: 354 us
  Pallas kernels  302 us (85%)
  matrix products  40.4 us (11%)
  local copies, waits for them, and re-layouts  8 us (2%)
    pallas_call x1, Pallas kernels, exchange(): pl.pallas_call(functools.partial(exchange_kernel, nrow, ncol, brows, bcol...  187 us
    pallas_call x1, Pallas kernels, spread(): pl.pallas_call(functools.partial(spread_kernel, nrow, ncol, width), out_s...  101 us
    dot_general x7, matrix products, matmul(): jnp.dot(left_side, right_side, preferred_element_type=jnp.float32, precis...  40.3 us
    pallas_call x1, Pallas kernels, gather_blocks(): pl.pallas_call(functools.partial(gather_kernel, count, bcols), out_shape=...  7.58 us

profile of v4, /device:TPU:7, one launch (start us, length us, event | category | flops | bytes accessed | tf_op | source)
XLA Modules:
  0.0 354.4 jit_solution(9779319338233498113)
XLA Ops:
  0.6 0.1 broadcast_in_dim.44
  0.7 0.1 broadcast_in_dim.45
  0.8 0.7 broadcast_add_fusion
  1.5 0.1 copy.17
  1.6 0.1 add.60
  1.7 0.8 copy.14
  2.5 0.1 eq.36
  2.6 0.1 convolution_convert_fusion
  2.7 0.2 fusion.24
  2.8 0.2 select_reduce_fusion
  3.1 0.1 copy.15
  3.2 0.1 reduce_or.12
  3.3 0.1 copy.20
  3.4 0.1 copy.16
  3.5 0.1 reduce_sum.21
  3.6 0.1 reshape.86
  3.7 0.6 fusion.25.where
  4.3 0.7 broadcast_in_dim.49.labels
  5.0 0.0 copy-start.5
  5.0 101.2 %spread.1 = (f32[2048,1024]{1,0:T(8,128)}, f32[1024,1024]{1,0:T(8,128)}, f32[2,512,512]{2,1,0:T(8,128)}) custom-call(f32[2048,1024]{1,0:T(8,128)} %front.1), custom_call_target="tpu_custom_call" | custom-call | tf_op jit(solution)/shard_map/spread/pallas_call | solution.py:271
  106.2 0.0 copy-start.4
  106.2 0.0 copy-done.5
  106.2 2.4 fusion.11
  108.6 3.7 %fusion.7 = f32[512,1024]{1,0:T(8,128)S(1)} fusion(f32[512,512]{1,0:T(8,128)S(1)} %fusion.11, f32[1024,1024]{1,0:T(8,128)} %get-tuple-element.9), kind=kOutput, calls=%fused_computation.8 | convolution fusion | flops 1610612736 | bytes 5242880 | tf_op jit(solution)/shard_map/dot_general | solution.py:17
  112.4 0.0 copy-done.4
  112.4 0.0 copy-start.7
  112.4 4.9 %fusion.3 = f32[2048,512]{0,1:T(8,128)S(1)} fusion(f32[2048,1024]{1,0:T(8,128)S(1)} %copy-done.4, f32[2,512,512]{2,1,0:T(8,128)} %param.6), kind=kOutput, calls=%fused_computation.4 | convolution fusion | flops 3221225472 | bytes 9437184 | tf_op jit(solution)/shard_map/dot_general | solution.py:17
  117.3 0.0 copy-done.7
  117.3 0.0 copy-start
  117.3 0.0 copy-start.6
  117.3 3.5 fusion.14
  120.8 0.0 copy-done.6
  120.8 3.8 %fusion = f32[2048,512]{0,1:T(8,128)S(1)} fusion(f32[2048,512]{1,0:T(8,128)S(1)} %fusion.14, f32[2048,1024]{1,0:T(8,128)S(1)} %copy-done.4, f32[2,512,512]{2,1,0:T(8,128)S(1)} %copy-done.6), kind=kOutput, calls=%fused_computation.1 | convolution fusion | flops 3222274048 | bytes 13631488 | tf_op jit(solution)/shard_map/dot_general | solution.py:17
  124.6 0.0 copy-done
  124.6 0.0 copy-start.1
  124.7 0.1 constant_dynamic-slice_fusion
  124.8 1.8 copy-done.1
  126.6 1.0 pad_maximum_fusion
  127.6 2.5 copy.19
  130.2 0.0 copy-start.2
  130.2 0.0 copy-start.3
  130.2 9.8 %fusion.9 = f32[2048,1024]{1,0:T(8,128)S(1)} fusion(f32[2048,512]{0,1:T(8,128)} %copy-done, f32[1024,1024]{1,0:T(8,128)} %get-tuple-element.9), kind=kOutput, calls=%fused_computation.10 | convolution fusion | flops 6442450944 | bytes 14680064 | tf_op jit(solution)/shard_map/dot_general | solution.py:17
  140.0 0.0 copy-done.2
  140.0 0.0 copy-done.3
  140.0 12.2 %subtract_subtract_fusion.updated = f32[2048,1024]{1,0:T(8,128)} fusion(f32[2048,1024]{1,0:T(8,128)} %front.1, f32[2048,1024]{1,0:T(8,128)S(1)} %fusion.9, f32[2048,512]{0,1:T(8,128)S(1)} %copy-done.2, f32[512,1024]{1,0:T(8,128)S(1)} %fusion.7, f32[1024,1024]{1,0:T(8,128)S(1)} %copy-done.3), kind=kOutput, calls=%fused_computation | convolution fusion | flops 6447169536 | bytes 33554432 | tf_op jit(solution)/shard_map/dot_general | solution.py:17
  152.2 7.6 %gather_blocks.1.blocks = f32[128,128,128]{2,1,0:T(8,128)} custom-call(s32[128]{0:T(128)} %fusion.25.where, f32[2048,1024]{1,0:T(8,128)} %subtract_subtract_fusion.updated), custom_call_target="tpu_custom_call" | custom-call | tf_op jit(solution)/shard_map/gather_blocks/pallas_call | solution.py:309
  159.8 186.8 %exchange.1 = (f32[128,128,128]{2,1,0:T(8,128)}, s32[32,8,128]{2,1,0:T(8,128)}) custom-call(f32[128,128,128]{2,1,0:T(8,128)} %gather_blocks.1.blocks, s32[32,8,128]{2,1,0:T(8,128)} %broadcast_in_dim.49.labels), custom_call_target="tpu_custom_call" | custom-call | tf_op jit(solution)/shard_map/exchange/pallas_call | solution.py:469
  346.6 0.9 slice_reduce_fusion
  347.5 0.1 squeeze.20
  347.6 0.5 broadcast_select_fusion.marks
  348.2 6.1 %add_blocks.1 = f32[48,128,128]{2,1,0:T(8,128)} custom-call(s32[128]{0:T(128)} %broadcast_select_fusion.marks, f32[48,128,128]{2,1,0:T(8,128)} %parent.1, f32[128,128,128]{2,1,0:T(8,128)} %get-tuple-element.12.arrived), custom_call_target="tpu_custom_call" | custom-call | tf_op jit(solution)/shard_map/add_blocks/pallas_call | solution.py:522
  (5 shorter events, 0.0 us)
Async XLA Ops:
  5.0 101.2 %copy-start.5 = (f32[2,512,512]{2,1,0:T(8,128)S(1)}, f32[2,512,512]{2,1,0:T(8,128)}, u32[]{:S(2)}) copy-start(f32[2,512,512]{2,1,0:T(8,128)} %param.6) | copy-start | bytes 6291460
  106.2 6.2 %copy-start.4 = (f32[2048,1024]{1,0:T(8,128)S(1)}, f32[2048,1024]{1,0:T(8,128)}, u32[]{:S(2)}) copy-start(f32[2048,1024]{1,0:T(8,128)} %get-tuple-element.8) | copy-start | bytes 25165828
  112.4 4.9 %copy-start.7 = (f32[2,512,512]{2,1,0:T(8,128)S(1)}, f32[2,512,512]{2,1,0:T(8,128)}, u32[]{:S(2)}) copy-start(f32[2,512,512]{2,1,0:T(8,128)} %get-tuple-element.10) | copy-start | bytes 6291460
  117.3 7.3 %copy-start = (f32[2048,512]{0,1:T(8,128)}, f32[2048,512]{0,1:T(8,128)S(1)}, u32[]{:S(2)}) copy-start(f32[2048,512]{0,1:T(8,128)S(1)} %fusion.3) | copy-start | bytes 12582916
  117.3 3.5 copy-start.6
  124.6 1.9 copy-start.1
  130.2 9.8 %copy-start.2 = (f32[2048,512]{0,1:T(8,128)S(1)}, f32[2048,512]{0,1:T(8,128)}, u32[]{:S(2)}) copy-start(f32[2048,512]{0,1:T(8,128)} %copy-done.1) | copy-start | bytes 12582916
  130.2 9.8 %copy-start.3 = (f32[1024,1024]{1,0:T(8,128)S(1)}, f32[1024,1024]{1,0:T(8,128)}, u32[]{:S(2)}) copy-start(f32[1024,1024]{1,0:T(8,128)} %get-tuple-element.9) | copy-start | bytes 12582916
